TPU v7x, 32 devices: a whole 2x2x4 slice. The times are simulated.
32 devices in a mesh: task: 16 (over z, y, x), shard: 2 (over core).
Axes of the slice: x: 2, y: 2, z: 4, core: 2. Of those that a mesh axis runs over, the one named last changes fastest.
Arguments:
- tokens: bfloat16 [16, 512, 1024], P('task'), may hold values from -6 to 6
- targets: bfloat16 [16, 512, 1024], P('task'), may hold values from -6 to 6
- meta_tokens: bfloat16 [16, 512, 1024], P('task'), may hold values from -6 to 6
- meta_targets: bfloat16 [16, 512, 1024], P('task'), may hold values from -6 to 6
- gate_weight: bfloat16 [16, 1024, 1536], P('task', None, 'shard'), may hold values from -0.1875 to 0.1875
- up_weight: bfloat16 [16, 1024, 1536], P('task', None, 'shard'), may hold values from -0.1875 to 0.1875
- down_weight: bfloat16 [16, 1536, 1024], P('task', 'shard'), may hold values from -0.15625 to 0.15625
- task_step: int32 [16], P('task'), may hold values from 0 to 9999
- hidden_state: float32 [16, 3, 512], P('task'), may hold values from -3 to 3
- cell_state: float32 [16, 3, 512], P('task'), may hold values from -6 to 6
- recurrent_weight: float32 [512, 2048], P('task'), may hold values from -0.25 to 0.25
- input_weight: float32 [3, 2048], replicated, may hold values from -3.5 to 3.5
- lstm_bias: float32 [2048], replicated, may hold values from -3 to 3
- context_weight: float32 [512, 5], replicated, may hold values from -0.25 to 0.25
- mlp_weight: float32 [3, 4], replicated, may hold values from -4 to 4
Outputs:
- gate_update: bfloat16 [16, 1024, 1536], P('task', None, 'shard')
- up_update: bfloat16 [16, 1024, 1536], P('task', None, 'shard')
- down_update: bfloat16 [16, 1536, 1024], P('task', 'shard')
- new_hidden: float32 [16, 3, 512], P('task')
- new_cell: float32 [16, 3, 512], P('task')
- meta_loss: float32 [], replicated
All inputs are finite; a program needn't handle non-finite values.
Results may differ from a plain program's by a relative error of at most 0.0056.
Values sent between devices are 32-bit elements; how exact they have to be, the bound alone decides.
A program may use at most 128 MiB of HBM per device.

v0:
```python
import jax
import jax.numpy as jnp
from jax import lax
from jax.sharding import PartitionSpec as P

STEPS = 10000
highest = lax.Precision.HIGHEST
epsilon = 1e-06
rate_factor = 0.1


def block_forward(inputs, w_gate, w_up, w_down):
    gate_pre = jnp.dot(inputs, w_gate, preferred_element_type=jnp.float32)
    up_pre = jnp.dot(inputs, w_up, preferred_element_type=jnp.float32)
    sigmoid_gate = jax.nn.sigmoid(gate_pre)
    activated = (gate_pre * sigmoid_gate * up_pre).astype(jnp.bfloat16)
    output = jnp.dot(activated, w_down, preferred_element_type=jnp.float32)
    return (gate_pre, up_pre, sigmoid_gate, activated, output)


def block_grads(inputs, w_down, gate_pre, up_pre, sigmoid_gate, activated, d_out):
    d_act = lax.dot_general(
        d_out, w_down, (((1,), (1,)), ((), ())), preferred_element_type=jnp.float32
    )
    d_gate = (d_act * up_pre * sigmoid_gate * (1.0 + gate_pre * (1.0 - sigmoid_gate))).astype(
        jnp.bfloat16
    )
    d_up = (d_act * gate_pre * sigmoid_gate).astype(jnp.bfloat16)
    grad_gate = lax.dot_general(
        inputs, d_gate, (((0,), (0,)), ((), ())), preferred_element_type=jnp.float32
    )
    grad_up = lax.dot_general(
        inputs, d_up, (((0,), (0,)), ((), ())), preferred_element_type=jnp.float32
    )
    grad_down = lax.dot_general(
        activated, d_out, (((0,), (0,)), ((), ())), preferred_element_type=jnp.float32
    )
    return (grad_gate, grad_up, grad_down)


def lstm_step(features, recurrent_term, cell_old, input_weight, lstm_bias, context_weight):
    state_width = cell_old.shape[-1]
    lstm_in = jnp.dot(features, input_weight, precision=highest) + recurrent_term + lstm_bias
    in_gate = jax.nn.sigmoid(lstm_in[:, :state_width])
    forget_gate = jax.nn.sigmoid(lstm_in[:, state_width : 2 * state_width])
    candidate = jnp.tanh(lstm_in[:, 2 * state_width : 3 * state_width])
    out_gate = jax.nn.sigmoid(lstm_in[:, 3 * state_width :])
    cell_new = forget_gate * cell_old + in_gate * candidate
    hidden_new = out_gate * jnp.tanh(cell_new)
    context = jnp.dot(hidden_new, context_weight, precision=highest)
    return (hidden_new, cell_new, context)


def param_update(param, gradient, rms_param, rms_grad, context_row, mlp_weight):
    p_norm = param.astype(jnp.float32) / rms_param
    g_norm = gradient / rms_grad
    summed = jnp.zeros(param.shape, jnp.float32)
    for hidden_unit in range(mlp_weight.shape[1]):
        inner = (
            mlp_weight[0, hidden_unit] * p_norm
            + mlp_weight[1, hidden_unit] * g_norm
            + context_row[hidden_unit]
        )
        summed = summed + mlp_weight[2, hidden_unit] * jax.nn.relu(inner)
    update = jnp.exp(context_row[-1]) * summed
    new_param = (param.astype(jnp.float32) - rate_factor * rms_param * update).astype(jnp.bfloat16)
    return (update.astype(jnp.bfloat16), new_param)


def local(
    tokens,
    targets,
    meta_tokens,
    meta_targets,
    gate_weight,
    up_weight,
    down_weight,
    task_step,
    hidden_state,
    cell_state,
    recurrent_weight,
    input_weight,
    lstm_bias,
    context_weight,
    mlp_weight,
):
    inputs = tokens[0]
    wanted = targets[0]
    meta_in = meta_tokens[0]
    meta_want = meta_targets[0]
    params = (gate_weight[0], up_weight[0], down_weight[0])
    gate_pre, up_pre, sigmoid_gate, activated, partial_out = block_forward(
        inputs, params[0], params[1], params[2]
    )
    output = lax.psum(partial_out, "shard")
    d_out = (output - wanted.astype(jnp.float32)).astype(jnp.bfloat16)
    gradients = block_grads(inputs, params[2], gate_pre, up_pre, sigmoid_gate, activated, d_out)
    grad_sq = jnp.stack([jnp.sum(grad_piece * grad_piece) for grad_piece in gradients])
    param_sq = jnp.stack(
        [jnp.sum(jnp.square(param_piece.astype(jnp.float32))) for param_piece in params]
    )
    tensor_sums = lax.psum(jnp.stack([grad_sq, param_sq]), "shard")
    entries = float(params[0].size * lax.axis_size("shard"))
    rms_grad = jnp.sqrt(tensor_sums[0] / entries + epsilon)
    rms_param = jnp.sqrt(tensor_sums[1] / entries + epsilon)
    fraction = jnp.full((3,), task_step[0].astype(jnp.float32) / STEPS, jnp.float32)
    features = jnp.stack([jnp.log(rms_grad), jnp.log(rms_param), fraction], axis=1)
    hidden_old = hidden_state[0]
    recurrent_term = jnp.dot(
        hidden_old, lax.all_gather(recurrent_weight, "task", axis=0, tiled=True), precision=highest
    )
    hidden_new, cell_new, context = lstm_step(
        features, recurrent_term, cell_state[0], input_weight, lstm_bias, context_weight
    )
    results = [
        param_update(
            params[tensor_id],
            gradients[tensor_id],
            rms_param[tensor_id],
            rms_grad[tensor_id],
            context[tensor_id],
            mlp_weight,
        )
        for tensor_id in range(3)
    ]
    meta_partial = block_forward(meta_in, results[0][1], results[1][1], results[2][1])[4]
    loss_scale = 0.5 / (meta_want.shape[0] * meta_want.shape[1])
    meta_share = lax.psum_scatter(meta_partial, "shard", scatter_dimension=1, tiled=True)
    share_cols = meta_share.shape[1]
    want_share = lax.dynamic_slice_in_dim(
        meta_want, lax.axis_index("shard") * share_cols, share_cols, 1
    )
    meta_part = loss_scale * jnp.sum(jnp.square(meta_share - want_share.astype(jnp.float32)))
    summed = lax.psum(meta_part, ("task", "shard"))
    meta_loss = summed / lax.axis_size("task")
    return (
        results[0][0][None],
        results[1][0][None],
        results[2][0][None],
        hidden_new[None],
        cell_new[None],
        meta_loss,
    )


def solution(mesh):
    return jax.shard_map(
        local,
        mesh=mesh,
        in_specs=(
            P("task", None, None),
            P("task", None, None),
            P("task", None, None),
            P("task", None, None),
            P("task", None, "shard"),
            P("task", None, "shard"),
            P("task", "shard", None),
            P("task"),
            P("task", None, None),
            P("task", None, None),
            P("task", None),
            P(),
            P(),
            P(),
            P(),
        ),
        out_specs=(
            P("task", None, "shard"),
            P("task", None, "shard"),
            P("task", "shard", None),
            P("task", None, None),
            P("task", None, None),
            P(),
        ),
        check_vma=False,
    )
```

profile of v0, /device:TPU:0, one launch (start us, length us, event | category | flops | bytes accessed | tf_op | source)
XLA Modules:
  0.0 225.3 jit_solution(7514482021820399542)
XLA Ops:
  9.2 2.4 %fusion.48 = f32[512,768]{1,0:T(8,128)S(1)} fusion(bf16[1,1024,768]{2,1,0:T(8,128)(2,1)} %param.19, bf16[1,512,1024]{2,1,0:T(8,128)(2,1)S(1)} %copy-done), kind=kOutput, calls=%fused_computation.68 | convolution fusion | flops 805306368 | bytes 4194304 | tf_op jit(solution)/shard_map/dot_general | solution.py:13
  11.7 2.1 multiply_convert_fusion.2
  13.8 2.3 %fusion.57 = f32[512,1024]{1,0:T(8,128)} fusion(bf16[512,768]{1,0:T(8,128)(2,1)S(1)} %get-tuple-element.57, bf16[1,768,1024]{2,1,0:T(8,128)(2,1)S(1)} %copy-done.4), kind=kOutput, calls=%fused_computation.80 | convolution fusion | flops 805306368 | bytes 4456448 | tf_op jit(solution)/shard_map/dot_general | solution.py:17
  16.8 1.7 copy.22
  18.5 2.6 %copy.21 = bf16[1,1024,768]{1,2,0:T(8,128)(2,1)} copy(bf16[1,1024,768]{2,1,0:T(8,128)(2,1)} %param.19) | data formatting | bytes 3145728 | tf_op args[4]
  22.6 2.8 %fusion.4 = f32[]{:T(128)} fusion(bf16[1,768,1024]{2,1,0:T(8,128)(2,1)} %param.21), kind=kLoop, calls=%fused_computation.13 | loop fusion | flops 2359295 | bytes 1572868 | tf_op jit(solution)/shard_map/reduce_sum | solution.py:100
  28.3 12.0 %all-reduce.2.cloned.1.call-done = f32[512,1024]{1,0:T(8,128)} async-done(((f32[512,1024]{1,0:T(8,128)}), f32[512,1024]{1,0:T(8,128)}) %all-reduce.2.cloned.1.call-update) | async-done | bytes 2097168 | tf_op jit(solution)/shard_map/psum | solution.py:95
  40.3 3.5 %fusion.55 = f32[512,768]{1,0:T(8,128)S(1)} fusion(bf16[1,768,1024]{2,1,0:T(8,128)(2,1)} %param.21, f32[512,1024]{1,0:T(8,128)} %all-reduce.2.cloned.1.call-done, bf16[1,512,1024]{2,1,0:T(8,128)(2,1)} %param.16), kind=kOutput, calls=%fused_computation.78 | convolution fusion | flops 806879232 | bytes 6291456 | tf_op jit(solution)/shard_map/dot_general | solution.py:22
  43.9 3.3 %multiply_reduce_fusion = (f32[]{:T(128)}, f32[768,1024]{1,0:T(8,128)}) fusion(bf16[512,768]{1,0:T(8,128)(2,1)S(1)} %get-tuple-element.57, f32[512,1024]{1,0:T(8,128)S(1)} %copy-done.6, bf16[1,512,1024]{2,1,0:T(8,128)(2,1)S(1)} %copy-done.8), kind=kOutput, calls=%fused_computation.56 | convolution fusion | flops 808452096 | bytes 7077892 | tf_op jit(solution)/shard_map/dot_general | solution.py:35
  47.3 3.5 %multiply_reduce_fusion.1 = (f32[]{:T(128)}, f32[768,1024]{1,0:T(8,128)}) fusion(bf16[1,512,1024]{2,1,0:T(8,128)(2,1)S(1)} %copy-done, f32[512,768]{1,0:T(8,128)S(1)} %fusion.55, f32[512,768]{1,0:T(8,128)S(1)} %copy-done.21), kind=kOutput, calls=%fused_computation.57 | convolution fusion | flops 809238528 | bytes 7340036 | tf_op jit(solution)/shard_map/dot_general | solution.py:32
  50.7 3.6 %multiply_reduce_fusion.2 = (f32[]{:T(128)}, f32[768,1024]{1,0:T(8,128)}) fusion(bf16[1,512,1024]{2,1,0:T(8,128)(2,1)S(1)} %copy-done, f32[512,768]{1,0:T(8,128)S(1)} %copy-done.21, f32[512,768]{1,0:T(8,128)S(1)} %fusion.55, f32[512,768]{1,0:T(8,128)S(1)} %copy-done.22), kind=kOutput, calls=%fused_computation.58 | convolution fusion | flops 810811392 | bytes 8912900 | tf_op jit(solution)/shard_map/dot_general | solution.py:29
  54.3 3.9 %maximum_bitcast_fusion = (f32[1,3]{1,0:T(1,128)S(1)}, f32[1,3]{1,0:T(1,128)S(1)}) fusion(f32[1]{0:T(128)} %bitcast.7, f32[1]{0:T(128)} %bitcast.6, f32[1]{0:T(128)} %bitcast.5, f32[1]{0:T(128)} %bitcast.11, f32[1]{0:T(128)} %bitcast.10, f32[1]{0:T(128)} %bitcast.9), kind=kLoop, calls=%fused_computation.130 | loop fusion | flops 12 | bytes 48 | tf_op jit(solution)/shard_map/stack | solution.py:102
  58.3 2.6 %psum.22 = f32[2,3]{1,0:T(2,128)S(1)} all-reduce(f32[2,3]{1,0:T(2,128)S(1)} %pad_maximum_fusion), channel_id=1, replica_groups=mesh['task'=16,'shard'=2] {'shard'}, use_global_device_ids=true, to_apply=%region_7.0 | all-reduce | flops 6 | bytes 48 | tf_op jit(solution)/shard_map/psum | solution.py:102
  64.3 33.4 %all-gather.2.cloned.1.call-done = f32[512,2048]{1,0:T(8,128)} async-done(((f32[32,2048]{1,0:T(8,128)}), f32[512,2048]{1,0:T(8,128)}) %all-gather.2.cloned.1.call-update) | async-done | bytes 4194320 | tf_op jit(solution)/shard_map/all_gather | solution.py:110
  97.7 4.4 %fusion.38 = f32[3,2048]{1,0:T(4,128)S(1)} fusion(f32[3,2048]{1,0:T(4,128)S(1)} %fusion.93, f32[512,2048]{1,0:T(8,128)} %all-gather.2.cloned.1.call-done, f32[2048]{0:T(1024)S(1)} %copy-done.18, f32[1,3,512]{2,0,1:T(1,128)S(1)} %copy-done.17), kind=kOutput, calls=%fused_computation.60 | convolution fusion | flops 37761024 | bytes 4257792 | tf_op jit(solution)/shard_map/dot_general | solution.py:109
  105.0 15.6 %convert_bitcast_fusion.1 = (bf16[1,1024,768]{1,2,0:T(8,128)(2,1)}, f32[1024,768]{0,1:T(8,128)S(1)}) fusion(f32[]{:T(128)} %bitcast.50, f32[]{:T(128)} %bitcast.36, f32[]{:T(128)} %bitcast.35, f32[]{:T(128)} %bitcast.34, f32[]{:T(128)} %bitcast.48, f32[]{:T(128)} %bitcast.31, f32[]{:T(128)} %bitcast.30, f32[]{:T(128)} %bitcast.29, f32[]{:T(128)} %bitcast.46, ...), kind=kLoop, calls=%fused_computation.88 | loop fusion | flops 25165824 | bytes 9437260 | tf_op jit(solution)/shard_map/broadcast_in_dim | solution.py:138
  120.6 2.3 %fusion.42 = f32[768,512]{0,1:T(8,128)} fusion(f32[1024,768]{0,1:T(8,128)S(1)} %get-tuple-element.15, bf16[1,1024,768]{1,2,0:T(8,128)(2,1)S(1)} %copy.22, f32[]{:T(128)S(6)} %mul.394, bf16[1,512,1024]{2,1,0:T(8,128)(2,1)S(1)} %copy-done.12), kind=kOutput, calls=%fused_computation.64 | convolution fusion | flops 808452096 | bytes 7340036 | tf_op jit(solution)/shard_map/dot_general | solution.py:14
  123.5 16.5 %convert_bitcast_fusion = (bf16[1,768,1024]{2,1,0:T(8,128)(2,1)}, f32[768,1024]{1,0:T(8,128)}) fusion(f32[]{:T(128)} %bitcast.58, f32[]{:T(128)} %bitcast.36, f32[]{:T(128)} %bitcast.35, f32[]{:T(128)} %bitcast.34, f32[]{:T(128)} %bitcast.57, f32[]{:T(128)} %bitcast.31, f32[]{:T(128)} %bitcast.30, f32[]{:T(128)} %bitcast.29, f32[]{:T(128)} %bitcast.56, ...), kind=kLoop, calls=%fused_computation.87 | loop fusion | flops 25165824 | bytes 9437260 | tf_op jit(solution)/shard_map/broadcast_in_dim | solution.py:139
  140.1 16.0 %convert_bitcast_fusion.2 = (bf16[1,1024,768]{1,2,0:T(8,128)(2,1)}, f32[1024,768]{0,1:T(8,128)}) fusion(f32[]{:T(128)} %bitcast.38, f32[]{:T(128)} %bitcast.36, f32[]{:T(128)} %bitcast.35, f32[]{:T(128)} %bitcast.34, f32[]{:T(128)} %bitcast.33, f32[]{:T(128)} %bitcast.31, f32[]{:T(128)} %bitcast.30, f32[]{:T(128)} %bitcast.29, f32[]{:T(128)} %bitcast.28, ...), kind=kLoop, calls=%fused_computation.89 | loop fusion | flops 25165824 | bytes 9437260 | tf_op jit(solution)/shard_map/broadcast_in_dim | solution.py:137
  156.1 7.8 %fusion.40 = f32[512,1024]{1,0:T(8,128)} fusion(f32[768,1024]{1,0:T(8,128)} %get-tuple-element.13, bf16[1,768,1024]{2,1,0:T(8,128)(2,1)} %param.21, f32[]{:T(128)S(6)} %mul.398, f32[768,512]{0,1:T(8,128)} %fusion.42, bf16[1,512,1024]{2,1,0:T(8,128)(2,1)} %param.17, f32[1024,768]{0,1:T(8,128)} %get-tuple-element.17, bf16[1,1024,768]{1,2,0:T(8,128)(2,1)S(1)} %copy-done.3, ...), kind=kOutput, calls=%fused_computation.63 | convolution fusion | flops 1619263488 | bytes 14155784 | tf_op jit(solution)/shard_map/dot_general | solution.py:17
  166.8 2.7 %copy.24 = bf16[1,1024,768]{2,1,0:T(8,128)(2,1)} copy(bf16[1,1024,768]{1,2,0:T(8,128)(2,1)} %get-tuple-element.16) | data formatting | bytes 3145728
  170.1 2.2 reduce-scatter.2.cloned.1.call-done
  172.3 2.1 fusion.65
  175.6 40.5 %psum.23 = f32[]{:T(128)} all-reduce(f32[]{:T(128)S(6)} %mul_shard_map.3), channel_id=1, replica_groups=mesh['task'=16,'shard'=2] {'task','shard'}, use_global_device_ids=true, to_apply=%region_10.11 | all-reduce | flops 1 | bytes 8 | tf_op jit(solution)/shard_map/psum | solution.py:134
  (67 shorter events, 12.9 us)
Async XLA Ops:
  8.0 3.6 %copy-start.11 = (bf16[1,1024,768]{2,1,0:T(8,128)(2,1)S(1)}, bf16[1,1024,768]{2,1,0:T(8,128)(2,1)}, u32[]{:S(2)}) copy-start(bf16[1,1024,768]{2,1,0:T(8,128)(2,1)} %param.20) | copy-start | bytes 4718596
  8.0 32.3 %all-reduce.2.cloned.1.call-start = ((), (), s32[]{:S(2)}) async-start(), calls=%async_computation.1 | async-start | bytes 4194304 | tf_op jit(solution)/shard_map/psum | solution.py:95
  11.6 2.2 copy-start.20
  11.6 2.2 copy-start.4
  16.2 81.5 %all-gather.2.cloned.1.call-start = ((), (), s32[]{:S(2)}) async-start(), calls=%async_computation.2 | async-start | bytes 4456448 | tf_op jit(solution)/shard_map/all_gather | solution.py:110
  16.7 5.1 %copy-start.15 = (f32[3,4]{1,0:T(4,128)S(1)}, f32[3,4]{1,0:T(4,128)}, u32[]{:S(2)}) copy-start(f32[3,4]{1,0:T(4,128)} %param.29) | copy-start | bytes 148
  16.8 155.5 %reduce-scatter.2.cloned.1.call-start = ((), (), s32[]{:S(2)}) async-start(), calls=%async_computation.3 | async-start | bytes 3145728 | tf_op jit(solution)/shard_map/reduce_scatter | solution.py:128
  21.1 5.7 %copy-start.2 = (bf16[1,1024,768]{1,2,0:T(8,128)(2,1)S(1)}, bf16[1,1024,768]{1,2,0:T(8,128)(2,1)}, u32[]{:S(2)}) copy-start(bf16[1,1024,768]{1,2,0:T(8,128)(2,1)} %copy.21) | copy-start | bytes 4718596
  40.3 3.5 %copy-start.6 = (f32[512,1024]{1,0:T(8,128)S(1)}, f32[512,1024]{1,0:T(8,128)}, u32[]{:S(2)}) copy-start(f32[512,1024]{1,0:T(8,128)} %all-reduce.2.cloned.1.call-done) | copy-start | bytes 6291460
  40.3 3.5 %copy-start.8 = (bf16[1,512,1024]{2,1,0:T(8,128)(2,1)S(1)}, bf16[1,512,1024]{2,1,0:T(8,128)(2,1)}, u32[]{:S(2)}) copy-start(bf16[1,512,1024]{2,1,0:T(8,128)(2,1)} %param.16) | copy-start | bytes 3145732
  43.9 3.4 %copy-start.21 = (f32[512,768]{1,0:T(8,128)S(1)}, f32[512,768]{1,0:T(8,128)}, u32[]{:S(2)}) copy-start(f32[512,768]{1,0:T(8,128)} %copy-done.20) | copy-start | bytes 4718596
  47.3 3.5 %copy-start.22 = (f32[512,768]{1,0:T(8,128)S(1)}, f32[512,768]{1,0:T(8,128)}, u32[]{:S(2)}) copy-start(f32[512,768]{1,0:T(8,128)} %get-tuple-element.58) | copy-start | bytes 4718596
  50.7 13.3 %copy-start.14 = (f32[3,2048]{1,0:T(4,128)S(1)}, f32[3,2048]{1,0:T(4,128)}, u32[]{:S(2)}) copy-start(f32[3,2048]{1,0:T(4,128)} %param.26) | copy-start | bytes 73732
  50.7 46.9 %copy-start.17 = (f32[1,3,512]{2,0,1:T(1,128)S(1)}, f32[1,3,512]{2,0,1:T(1,128)}, u32[]{:S(2)}) copy-start(f32[1,3,512]{2,0,1:T(1,128)} %param.23) | copy-start | bytes 18436
  50.7 46.9 %copy-start.18 = (f32[2048]{0:T(1024)S(1)}, f32[2048]{0:T(1024)}, u32[]{:S(2)}) copy-start(f32[2048]{0:T(1024)} %param.27) | copy-start | bytes 24580
  54.3 47.7 %copy-start.19 = (f32[1,3,512]{2,0,1:T(1,128)S(1)}, f32[1,3,512]{2,0,1:T(1,128)}, u32[]{:S(2)}) copy-start(f32[1,3,512]{2,0,1:T(1,128)} %param.24) | copy-start | bytes 18436
  54.3 47.8 %copy-start.16 = (f32[512,5]{0,1:T(8,128)S(1)}, f32[512,5]{0,1:T(8,128)}, u32[]{:S(2)}) copy-start(f32[512,5]{0,1:T(8,128)} %param.28) | copy-start | bytes 30724
  97.7 7.3 %copy-start.10 = (f32[768,1024]{1,0:T(8,128)S(1)}, f32[768,1024]{1,0:T(8,128)}, u32[]{:S(2)}) copy-start(f32[768,1024]{1,0:T(8,128)} %get-tuple-element.62) | copy-start | bytes 9437188
  105.0 15.6 %copy-start.12 = (bf16[1,512,1024]{2,1,0:T(8,128)(2,1)S(1)}, bf16[1,512,1024]{2,1,0:T(8,128)(2,1)}, u32[]{:S(2)}) copy-start(bf16[1,512,1024]{2,1,0:T(8,128)(2,1)} %param.17) | copy-start | bytes 3145732
  120.6 2.3 %copy-start.1 = (f32[768,1024]{1,0:T(8,128)S(1)}, f32[768,1024]{1,0:T(8,128)}, u32[]{:S(2)}) copy-start(f32[768,1024]{1,0:T(8,128)} %get-tuple-element.60) | copy-start | bytes 9437188
  120.6 2.9 %copy-start.5 = (bf16[1,768,1024]{2,1,0:T(8,128)(2,1)S(1)}, bf16[1,768,1024]{2,1,0:T(8,128)(2,1)}, u32[]{:S(2)}) copy-start(bf16[1,768,1024]{2,1,0:T(8,128)(2,1)} %param.21) | copy-start | bytes 4718596
  123.5 16.6 %copy-start.3 = (bf16[1,1024,768]{1,2,0:T(8,128)(2,1)S(1)}, bf16[1,1024,768]{1,2,0:T(8,128)(2,1)}, u32[]{:S(2)}) copy-start(bf16[1,1024,768]{1,2,0:T(8,128)(2,1)} %copy.21) | copy-start | bytes 4718596
  123.5 16.6 %copy-start.9 = (f32[768,1024]{1,0:T(8,128)S(1)}, f32[768,1024]{1,0:T(8,128)}, u32[]{:S(2)}) copy-start(f32[768,1024]{1,0:T(8,128)} %get-tuple-element.64) | copy-start | bytes 9437188
  166.8 5.4 %copy-start.13 = (bf16[1,512,1024]{2,1,0:T(8,128)(2,1)S(1)}, bf16[1,512,1024]{2,1,0:T(8,128)(2,1)}, u32[]{:S(2)}) copy-start(bf16[1,512,1024]{2,1,0:T(8,128)(2,1)} %param.18) | copy-start | bytes 3145732
  (2 other events, 2.6 us)
Sparse Core Ops, SparseCore 0:
  16.3 24.0 all-reduce.1
  164.0 8.2 reduce-scatter.1
Sparse Core Ops, SparseCore 1:
  19.4 78.2 all-gather.1
where the time goes:
time: 226 us; the launch traced here: 225 us
  other arithmetic  59.9 us (27%)
  waiting for transfers between devices  48.1 us (21%)
  blocking collectives  43.1 us (19%)
  matrix products  35.7 us (16%)
  between operations  22.6 us (10%)
  local copies, waits for them, and re-layouts  15.8 us (7%)
    psum x1, blocking collectives, local(): summed = lax.psum(meta_part, ('task', 'shard'))  40.5 us
    all_gather x1, waiting for transfers between devices, local(): lax.all_gather(recurrent_weight, 'task', axis=0, tiled=True)  33.4 us
    broadcast_in_dim x1, other arithmetic, local(): results[2][0][None]  16.5 us
    broadcast_in_dim x1, other arithmetic, local(): results[0][0][None]  16 us
    broadcast_in_dim x1, other arithmetic, local(): results[1][0][None]  15.6 us
    unnamed x52, local copies, waits for them, and re-layouts  13 us
    psum x1, waiting for transfers between devices, local(): output = lax.psum(partial_out, 'shard')  12 us
    dot_general x2, matrix products, block_forward(): output = jnp.dot(activated, w_down, preferred_element_type=jnp.float32)  10.1 us
  transfers between devices with their start and end apart: 3, of which 3 were waited for; matrix products, arithmetic and copies ran while one was open for 16% of the time, Pallas kernels for 0%

commit v1 on v0

--- a/solution.py
+++ b/solution.py
@@ -131,7 +131,7 @@
         meta_want, lax.axis_index("shard") * share_cols, share_cols, 1
     )
     meta_part = loss_scale * jnp.sum(jnp.square(meta_share - want_share.astype(jnp.float32)))
-    summed = lax.psum(meta_part, ("task", "shard"))
+    summed = lax.psum(lax.psum(meta_part, "shard"), "task")
     meta_loss = summed / lax.axis_size("task")
     return (
         results[0][0][None],

time: 226 us -> 232 us (1.027)
  blocking collectives: 43.1 us -> 48.3 us
    psum x1 -> x2, blocking collectives: 40.5 us -> 45.6 us  [local(): summed = lax.psum(lax.psum(meta_part, 'shard'), 'task')]
  transfers between devices with their start and end apart: 3 -> 3, of which waited for: 3 -> 3; matrix products, arithmetic and copies ran while one was open for 16% -> 15% of each run, Pallas kernels for 0% -> 0%
where the time goes in v1:
time: 232 us; the launch traced here: 231 us
  other arithmetic  59.7 us (26%)
  blocking collectives  48.3 us (21%)
  waiting for transfers between devices  48.2 us (21%)
  matrix products  35.7 us (15%)
  between operations  22.8 us (10%)
  local copies, waits for them, and re-layouts  15.9 us (7%)
    psum x2, blocking collectives, local(): summed = lax.psum(lax.psum(meta_part, 'shard'), 'task')  45.6 us
    all_gather x1, waiting for transfers between devices, local(): lax.all_gather(recurrent_weight, 'task', axis=0, tiled=True)  33 us
    broadcast_in_dim x1, other arithmetic, local(): results[2][0][None]  16.4 us
    broadcast_in_dim x1, other arithmetic, local(): results[0][0][None]  16 us
    broadcast_in_dim x1, other arithmetic, local(): results[1][0][None]  15.3 us
    unnamed x52, local copies, waits for them, and re-layouts  13 us
    psum x1, waiting for transfers between devices, local(): output = lax.psum(partial_out, 'shard')  11.9 us
    dot_general x2, matrix products, block_forward(): output = jnp.dot(activated, w_down, preferred_element_type=jnp.float32)  10.1 us
  transfers between devices with their start and end apart: 3, of which 3 were waited for; matrix products, arithmetic and copies ran while one was open for 15% of the time, Pallas kernels for 0%

profile of v1, /device:TPU:0, one launch (start us, length us, event | category | flops | bytes accessed | tf_op | source)
XLA Modules:
  0.0 230.7 jit_solution(17627008472409063550)
XLA Ops:
  9.2 2.4 %fusion.48 = f32[512,768]{1,0:T(8,128)S(1)} fusion(bf16[1,1024,768]{2,1,0:T(8,128)(2,1)} %param.19, bf16[1,512,1024]{2,1,0:T(8,128)(2,1)S(1)} %copy-done), kind=kOutput, calls=%fused_computation.68 | convolution fusion | flops 805306368 | bytes 4194304 | tf_op jit(solution)/shard_map/dot_general | solution.py:13
  11.7 2.1 multiply_convert_fusion.2
  13.8 2.3 %fusion.57 = f32[512,1024]{1,0:T(8,128)} fusion(bf16[512,768]{1,0:T(8,128)(2,1)S(1)} %get-tuple-element.57, bf16[1,768,1024]{2,1,0:T(8,128)(2,1)S(1)} %copy-done.4), kind=kOutput, calls=%fused_computation.80 | convolution fusion | flops 805306368 | bytes 4456448 | tf_op jit(solution)/shard_map/dot_general | solution.py:17
  18.5 2.6 %copy.21 = bf16[1,1024,768]{1,2,0:T(8,128)(2,1)} copy(bf16[1,1024,768]{2,1,0:T(8,128)(2,1)} %param.19) | data formatting | bytes 3145728 | tf_op args[4]
  22.6 2.9 %fusion.4 = f32[]{:T(128)} fusion(bf16[1,768,1024]{2,1,0:T(8,128)(2,1)} %param.21), kind=kLoop, calls=%fused_computation.13 | loop fusion | flops 2359295 | bytes 1572868 | tf_op jit(solution)/shard_map/reduce_sum | solution.py:100
  28.5 11.9 %all-reduce.2.cloned.1.call-done = f32[512,1024]{1,0:T(8,128)} async-done(((f32[512,1024]{1,0:T(8,128)}), f32[512,1024]{1,0:T(8,128)}) %all-reduce.2.cloned.1.call-update) | async-done | bytes 2097168 | tf_op jit(solution)/shard_map/psum | solution.py:95
  40.3 3.5 %fusion.55 = f32[512,768]{1,0:T(8,128)S(1)} fusion(bf16[1,768,1024]{2,1,0:T(8,128)(2,1)} %param.21, f32[512,1024]{1,0:T(8,128)} %all-reduce.2.cloned.1.call-done, bf16[1,512,1024]{2,1,0:T(8,128)(2,1)} %param.16), kind=kOutput, calls=%fused_computation.78 | convolution fusion | flops 806879232 | bytes 6291456 | tf_op jit(solution)/shard_map/dot_general | solution.py:22
  43.9 3.3 %multiply_reduce_fusion = (f32[]{:T(128)}, f32[768,1024]{1,0:T(8,128)}) fusion(bf16[512,768]{1,0:T(8,128)(2,1)S(1)} %get-tuple-element.57, f32[512,1024]{1,0:T(8,128)S(1)} %copy-done.6, bf16[1,512,1024]{2,1,0:T(8,128)(2,1)S(1)} %copy-done.8), kind=kOutput, calls=%fused_computation.56 | convolution fusion | flops 808452096 | bytes 7077892 | tf_op jit(solution)/shard_map/dot_general | solution.py:35
  47.3 3.4 %multiply_reduce_fusion.1 = (f32[]{:T(128)}, f32[768,1024]{1,0:T(8,128)}) fusion(bf16[1,512,1024]{2,1,0:T(8,128)(2,1)S(1)} %copy-done, f32[512,768]{1,0:T(8,128)S(1)} %fusion.55, f32[512,768]{1,0:T(8,128)S(1)} %copy-done.21), kind=kOutput, calls=%fused_computation.57 | convolution fusion | flops 809238528 | bytes 7340036 | tf_op jit(solution)/shard_map/dot_general | solution.py:32
  50.7 3.6 %multiply_reduce_fusion.2 = (f32[]{:T(128)}, f32[768,1024]{1,0:T(8,128)}) fusion(bf16[1,512,1024]{2,1,0:T(8,128)(2,1)S(1)} %copy-done, f32[512,768]{1,0:T(8,128)S(1)} %copy-done.21, f32[512,768]{1,0:T(8,128)S(1)} %fusion.55, f32[512,768]{1,0:T(8,128)S(1)} %copy-done.22), kind=kOutput, calls=%fused_computation.58 | convolution fusion | flops 810811392 | bytes 8912900 | tf_op jit(solution)/shard_map/dot_general | solution.py:29
  54.3 4.0 %maximum_bitcast_fusion = (f32[1,3]{1,0:T(1,128)S(1)}, f32[1,3]{1,0:T(1,128)S(1)}) fusion(f32[1]{0:T(128)} %bitcast.7, f32[1]{0:T(128)} %bitcast.6, f32[1]{0:T(128)} %bitcast.5, f32[1]{0:T(128)} %bitcast.11, f32[1]{0:T(128)} %bitcast.10, f32[1]{0:T(128)} %bitcast.9), kind=kLoop, calls=%fused_computation.130 | loop fusion | flops 12 | bytes 48 | tf_op jit(solution)/shard_map/stack | solution.py:102
  58.4 2.6 %psum.29 = f32[2,3]{1,0:T(2,128)S(1)} all-reduce(f32[2,3]{1,0:T(2,128)S(1)} %pad_maximum_fusion), channel_id=1, replica_groups=mesh['task'=16,'shard'=2] {'shard'}, use_global_device_ids=true, to_apply=%region_7.0 | all-reduce | flops 6 | bytes 48 | tf_op jit(solution)/shard_map/psum | solution.py:102
  64.6 33.0 %all-gather.2.cloned.1.call-done = f32[512,2048]{1,0:T(8,128)} async-done(((f32[32,2048]{1,0:T(8,128)}), f32[512,2048]{1,0:T(8,128)}) %all-gather.2.cloned.1.call-update) | async-done | bytes 4194320 | tf_op jit(solution)/shard_map/all_gather | solution.py:110
  97.6 4.4 %fusion.38 = f32[3,2048]{1,0:T(4,128)S(1)} fusion(f32[3,2048]{1,0:T(4,128)S(1)} %fusion.93, f32[512,2048]{1,0:T(8,128)} %all-gather.2.cloned.1.call-done, f32[2048]{0:T(1024)S(1)} %copy-done.18, f32[1,3,512]{2,0,1:T(1,128)S(1)} %copy-done.17), kind=kOutput, calls=%fused_computation.60 | convolution fusion | flops 37761024 | bytes 4257792 | tf_op jit(solution)/shard_map/dot_general | solution.py:109
  105.1 15.3 %convert_bitcast_fusion.1 = (bf16[1,1024,768]{1,2,0:T(8,128)(2,1)}, f32[1024,768]{0,1:T(8,128)S(1)}) fusion(f32[]{:T(128)} %bitcast.50, f32[]{:T(128)} %bitcast.36, f32[]{:T(128)} %bitcast.35, f32[]{:T(128)} %bitcast.34, f32[]{:T(128)} %bitcast.48, f32[]{:T(128)} %bitcast.31, f32[]{:T(128)} %bitcast.30, f32[]{:T(128)} %bitcast.29, f32[]{:T(128)} %bitcast.46, ...), kind=kLoop, calls=%fused_computation.88 | loop fusion | flops 25165824 | bytes 9437260 | tf_op jit(solution)/shard_map/broadcast_in_dim | solution.py:138
  120.4 2.3 fusion.42
  123.3 16.4 %convert_bitcast_fusion = (bf16[1,768,1024]{2,1,0:T(8,128)(2,1)}, f32[768,1024]{1,0:T(8,128)}) fusion(f32[]{:T(128)} %bitcast.58, f32[]{:T(128)} %bitcast.36, f32[]{:T(128)} %bitcast.35, f32[]{:T(128)} %bitcast.34, f32[]{:T(128)} %bitcast.57, f32[]{:T(128)} %bitcast.31, f32[]{:T(128)} %bitcast.30, f32[]{:T(128)} %bitcast.29, f32[]{:T(128)} %bitcast.56, ...), kind=kLoop, calls=%fused_computation.87 | loop fusion | flops 25165824 | bytes 9437260 | tf_op jit(solution)/shard_map/broadcast_in_dim | solution.py:139
  139.7 16.0 %convert_bitcast_fusion.2 = (bf16[1,1024,768]{1,2,0:T(8,128)(2,1)}, f32[1024,768]{0,1:T(8,128)}) fusion(f32[]{:T(128)} %bitcast.38, f32[]{:T(128)} %bitcast.36, f32[]{:T(128)} %bitcast.35, f32[]{:T(128)} %bitcast.34, f32[]{:T(128)} %bitcast.33, f32[]{:T(128)} %bitcast.31, f32[]{:T(128)} %bitcast.30, f32[]{:T(128)} %bitcast.29, f32[]{:T(128)} %bitcast.28, ...), kind=kLoop, calls=%fused_computation.89 | loop fusion | flops 25165824 | bytes 9437260 | tf_op jit(solution)/shard_map/broadcast_in_dim | solution.py:137
  155.7 7.8 %fusion.40 = f32[512,1024]{1,0:T(8,128)} fusion(f32[768,1024]{1,0:T(8,128)} %get-tuple-element.13, bf16[1,768,1024]{2,1,0:T(8,128)(2,1)} %param.21, f32[]{:T(128)S(6)} %mul.398, f32[768,512]{0,1:T(8,128)} %fusion.42, bf16[1,512,1024]{2,1,0:T(8,128)(2,1)} %param.17, f32[1024,768]{0,1:T(8,128)} %get-tuple-element.17, bf16[1,1024,768]{1,2,0:T(8,128)(2,1)S(1)} %copy-done.3, ...), kind=kOutput, calls=%fused_computation.63 | convolution fusion | flops 1619263488 | bytes 14155784 | tf_op jit(solution)/shard_map/dot_general | solution.py:17
  166.5 2.7 %copy.24 = bf16[1,1024,768]{2,1,0:T(8,128)(2,1)} copy(bf16[1,1024,768]{1,2,0:T(8,128)(2,1)} %get-tuple-element.16) | data formatting | bytes 3145728
  169.1 2.8 %reduce-scatter.2.cloned.1.call-done = f32[512,512]{1,0:T(8,128)} async-done(((f32[512,1024]{1,0:T(8,128)}), f32[512,512]{1,0:T(8,128)}) %reduce-scatter.2.cloned.1.call-update) | async-done | bytes 1048592 | tf_op jit(solution)/shard_map/reduce_scatter | solution.py:128
  171.9 2.1 fusion.65
  175.3 3.0 %psum.30 = f32[]{:T(128)} all-reduce(f32[]{:T(128)S(6)} %mul_shard_map.3), channel_id=1, replica_groups=mesh['task'=16,'shard'=2] {'shard'}, use_global_device_ids=true, to_apply=%region_10.11 | all-reduce | flops 1 | bytes 8 | tf_op jit(solution)/shard_map/psum | solution.py:134
  178.8 42.7 %psum.31 = f32[]{:T(128)} all-reduce(f32[]{:T(128)} %psum.30), channel_id=1, replica_groups=mesh['task'=16,'shard'=2] {'task'}, use_global_device_ids=true, to_apply=%region_11.12 | all-reduce | flops 1 | bytes 8 | tf_op jit(solution)/shard_map/psum | solution.py:134
  (68 shorter events, 14.7 us)
Async XLA Ops:
  8.0 3.6 %copy-start.11 = (bf16[1,1024,768]{2,1,0:T(8,128)(2,1)S(1)}, bf16[1,1024,768]{2,1,0:T(8,128)(2,1)}, u32[]{:S(2)}) copy-start(bf16[1,1024,768]{2,1,0:T(8,128)(2,1)} %param.20) | copy-start | bytes 4718596
  8.0 32.3 %all-reduce.2.cloned.1.call-start = ((), (), s32[]{:S(2)}) async-start(), calls=%async_computation.1 | async-start | bytes 4194304 | tf_op jit(solution)/shard_map/psum | solution.py:95
  11.6 2.2 copy-start.20
  11.6 2.2 copy-start.4
  16.2 81.5 %all-gather.2.cloned.1.call-start = ((), (), s32[]{:S(2)}) async-start(), calls=%async_computation.2 | async-start | bytes 4456448 | tf_op jit(solution)/shard_map/all_gather | solution.py:110
  16.7 5.1 %copy-start.15 = (f32[3,4]{1,0:T(4,128)S(1)}, f32[3,4]{1,0:T(4,128)}, u32[]{:S(2)}) copy-start(f32[3,4]{1,0:T(4,128)} %param.29) | copy-start | bytes 148
  16.8 155.2 %reduce-scatter.2.cloned.1.call-start = ((), (), s32[]{:S(2)}) async-start(), calls=%async_computation.3 | async-start | bytes 3145728 | tf_op jit(solution)/shard_map/reduce_scatter | solution.py:128
  21.1 5.9 %copy-start.2 = (bf16[1,1024,768]{1,2,0:T(8,128)(2,1)S(1)}, bf16[1,1024,768]{1,2,0:T(8,128)(2,1)}, u32[]{:S(2)}) copy-start(bf16[1,1024,768]{1,2,0:T(8,128)(2,1)} %copy.21) | copy-start | bytes 4718596
  40.3 3.5 %copy-start.6 = (f32[512,1024]{1,0:T(8,128)S(1)}, f32[512,1024]{1,0:T(8,128)}, u32[]{:S(2)}) copy-start(f32[512,1024]{1,0:T(8,128)} %all-reduce.2.cloned.1.call-done) | copy-start | bytes 6291460
  40.3 3.5 %copy-start.8 = (bf16[1,512,1024]{2,1,0:T(8,128)(2,1)S(1)}, bf16[1,512,1024]{2,1,0:T(8,128)(2,1)}, u32[]{:S(2)}) copy-start(bf16[1,512,1024]{2,1,0:T(8,128)(2,1)} %param.16) | copy-start | bytes 3145732
  43.9 3.4 %copy-start.21 = (f32[512,768]{1,0:T(8,128)S(1)}, f32[512,768]{1,0:T(8,128)}, u32[]{:S(2)}) copy-start(f32[512,768]{1,0:T(8,128)} %copy-done.20) | copy-start | bytes 4718596
  47.2 3.4 %copy-start.22 = (f32[512,768]{1,0:T(8,128)S(1)}, f32[512,768]{1,0:T(8,128)}, u32[]{:S(2)}) copy-start(f32[512,768]{1,0:T(8,128)} %get-tuple-element.58) | copy-start | bytes 4718596
  50.7 13.6 %copy-start.14 = (f32[3,2048]{1,0:T(4,128)S(1)}, f32[3,2048]{1,0:T(4,128)}, u32[]{:S(2)}) copy-start(f32[3,2048]{1,0:T(4,128)} %param.26) | copy-start | bytes 73732
  50.7 46.9 %copy-start.17 = (f32[1,3,512]{2,0,1:T(1,128)S(1)}, f32[1,3,512]{2,0,1:T(1,128)}, u32[]{:S(2)}) copy-start(f32[1,3,512]{2,0,1:T(1,128)} %param.23) | copy-start | bytes 18436
  50.7 46.9 %copy-start.18 = (f32[2048]{0:T(1024)S(1)}, f32[2048]{0:T(1024)}, u32[]{:S(2)}) copy-start(f32[2048]{0:T(1024)} %param.27) | copy-start | bytes 24580
  54.3 47.8 %copy-start.19 = (f32[1,3,512]{2,0,1:T(1,128)S(1)}, f32[1,3,512]{2,0,1:T(1,128)}, u32[]{:S(2)}) copy-start(f32[1,3,512]{2,0,1:T(1,128)} %param.24) | copy-start | bytes 18436
  54.3 47.8 %copy-start.16 = (f32[512,5]{0,1:T(8,128)S(1)}, f32[512,5]{0,1:T(8,128)}, u32[]{:S(2)}) copy-start(f32[512,5]{0,1:T(8,128)} %param.28) | copy-start | bytes 30724
  97.6 7.4 %copy-start.10 = (f32[768,1024]{1,0:T(8,128)S(1)}, f32[768,1024]{1,0:T(8,128)}, u32[]{:S(2)}) copy-start(f32[768,1024]{1,0:T(8,128)} %get-tuple-element.62) | copy-start | bytes 9437188
  105.1 15.3 %copy-start.12 = (bf16[1,512,1024]{2,1,0:T(8,128)(2,1)S(1)}, bf16[1,512,1024]{2,1,0:T(8,128)(2,1)}, u32[]{:S(2)}) copy-start(bf16[1,512,1024]{2,1,0:T(8,128)(2,1)} %param.17) | copy-start | bytes 3145732
  120.4 2.3 copy-start.1
  120.4 2.9 %copy-start.5 = (bf16[1,768,1024]{2,1,0:T(8,128)(2,1)S(1)}, bf16[1,768,1024]{2,1,0:T(8,128)(2,1)}, u32[]{:S(2)}) copy-start(bf16[1,768,1024]{2,1,0:T(8,128)(2,1)} %param.21) | copy-start | bytes 4718596
  123.3 16.4 %copy-start.3 = (bf16[1,1024,768]{1,2,0:T(8,128)(2,1)S(1)}, bf16[1,1024,768]{1,2,0:T(8,128)(2,1)}, u32[]{:S(2)}) copy-start(bf16[1,1024,768]{1,2,0:T(8,128)(2,1)} %copy.21) | copy-start | bytes 4718596
  123.3 16.4 %copy-start.9 = (f32[768,1024]{1,0:T(8,128)S(1)}, f32[768,1024]{1,0:T(8,128)}, u32[]{:S(2)}) copy-start(f32[768,1024]{1,0:T(8,128)} %get-tuple-element.64) | copy-start | bytes 9437188
  166.5 5.4 %copy-start.13 = (bf16[1,512,1024]{2,1,0:T(8,128)(2,1)S(1)}, bf16[1,512,1024]{2,1,0:T(8,128)(2,1)}, u32[]{:S(2)}) copy-start(bf16[1,512,1024]{2,1,0:T(8,128)(2,1)} %param.18) | copy-start | bytes 3145732
  (2 other events, 2.6 us)
Sparse Core Ops, SparseCore 0:
  16.3 24.0 all-reduce.1
  163.7 8.2 reduce-scatter.1
Sparse Core Ops, SparseCore 1:
  19.4 78.2 all-gather.1
